TPU v7x, 256 devices: a whole 4x4x8 slice. The times are simulated.
256 devices in a mesh: kq: 128 (over x, y, z), band: 2 (over core).
Axes of the slice: x: 4, y: 4, z: 8, core: 2. Of those that a mesh axis runs over, the one named last changes fastest.
Arguments:
- orbitals: bfloat16 [128, 16, 4096], P('kq', 'band'), may hold values from -6 to 6
- screening: bfloat16 [256, 1024, 1024], P('kq'), may hold values from -0.1875 to 0.1875
- pair_k: int32 [256, 2], replicated, may hold values from 0 to 127, as said below
- pair_q: int32 [256], P('kq'), may hold values from 0 to 255, as said below
- gmap: int32 [1024], replicated, may hold values from 0 to 4095, as said below
Outputs:
- exch_field: float32 [128, 16, 4096], P('kq', 'band')
Inputs may be any that keep to these rules, and one draw needn't show every extreme that they name: Rows are grouped by owner: rows o * 2 to (o + 1) * 2 - 1 belong to kq index o, and pair_k[o * 2 + i, s] = (pair_k[i, s] + o) mod 128 for every row i of owner 0 and both columns s. The 2 * 2 k-points of one owner are all different, and those of owner 0 include 128 - 1 and 64. `pair_q`: row i names one of the 2 transfers of owner o = i // 2, namely 2 * o to 2 * o + 1, and each of them in 1 of the owner's rows. `gmap`: all entries differ; 0 and 4095 are among them.
All inputs are finite; a program needn't handle non-finite values.
Results may differ from a plain program's by a relative error of at most 0.007.
Values may be sent and summed in bfloat16 or wider, within the bound.
A program may use at most 128 MiB of HBM per device.

v0:
```python
import math

import jax
import jax.numpy as jnp
from jax import lax
from jax.sharding import PartitionSpec as P

GRID = 16


def cas_table(gmap, grid_side):
    cells = grid_side**3
    points = jnp.arange(cells, dtype=jnp.int32)
    coord_x = points // (grid_side * grid_side)
    coord_y = points // grid_side % grid_side
    coord_z = points % grid_side
    freq_x = gmap // (grid_side * grid_side)
    freq_y = gmap // grid_side % grid_side
    freq_z = gmap % grid_side
    phase = (
        freq_x[:, None] * coord_x[None, :]
        + freq_y[:, None] * coord_y[None, :]
        + freq_z[:, None] * coord_z[None, :]
    ) % grid_side
    angle = phase.astype(jnp.float32) * (2.0 * math.pi / grid_side)
    return (jnp.cos(angle) + jnp.sin(angle)).astype(jnp.bfloat16)


def pair_fields(left_block, right_block, screen_mat, table):
    rows_left = left_block.shape[0]
    rows_right = right_block.shape[0]
    cells = table.shape[1]
    factor = 1.0 / math.sqrt(cells)
    density = (
        left_block.astype(jnp.float32)[:, None, :] * right_block.astype(jnp.float32)[None, :, :]
    ).astype(jnp.bfloat16)
    density = density.reshape(rows_left * rows_right, cells)
    spectrum = lax.dot_general(
        density, table, (((1,), (1,)), ((), ())), preferred_element_type=jnp.float32
    )
    spectrum = (spectrum * factor).astype(jnp.bfloat16)
    screened = jnp.dot(spectrum, screen_mat, preferred_element_type=jnp.float32).astype(
        jnp.bfloat16
    )
    potential = (jnp.dot(screened, table, preferred_element_type=jnp.float32) * factor).astype(
        jnp.bfloat16
    )
    potential = potential.reshape(rows_left, rows_right, cells)
    toward_left = jnp.einsum(
        "mnr,nr->mr", potential, right_block, preferred_element_type=jnp.float32
    )
    toward_right = jnp.einsum(
        "mnr,mr->nr", potential, left_block, preferred_element_type=jnp.float32
    )
    return (toward_left, toward_right)


def shards(orbitals, screening, pair_k, pair_q, gmap):
    owner_index = lax.axis_index("kq")
    pair_count = pair_q.shape[0]
    local_pairs = lax.dynamic_slice_in_dim(pair_k, owner_index * pair_count, pair_count, 0)
    first_points = local_pairs[:, 0]
    second_points = local_pairs[:, 1]
    shard_piece = lax.all_gather(orbitals, "kq", axis=0, tiled=True)
    numbers = jnp.arange(shard_piece.shape[0], dtype=jnp.int32)
    pick_first = (first_points[:, None] == numbers[None, :]).astype(jnp.bfloat16)
    pick_second = (second_points[:, None] == numbers[None, :]).astype(jnp.bfloat16)
    first_add = jnp.einsum(
        "pc,cnr->pnr", pick_first, shard_piece, preferred_element_type=jnp.float32
    )
    second_add = jnp.einsum(
        "pc,cnr->pnr", pick_second, shard_piece, preferred_element_type=jnp.float32
    )
    first_half = first_add.astype(jnp.bfloat16)
    second_half = second_add.astype(jnp.bfloat16)
    first_full = lax.all_gather(first_half, "band", axis=1, tiled=True)
    table = cas_table(gmap, GRID)
    screen_slots = pair_q - owner_index * screening.shape[0]

    def one_pair(operands):
        left_block, right_block, screen_slot = operands
        screen_mat = lax.dynamic_index_in_dim(screening, screen_slot, 0, keepdims=False)
        return pair_fields(left_block, right_block, screen_mat, table)

    toward_first, toward_second = lax.map(one_pair, (first_full, second_half, screen_slots))
    first_share = lax.psum_scatter(
        toward_first.astype(jnp.bfloat16), "band", scatter_dimension=1, tiled=True
    ).astype(jnp.float32)
    numbers = jnp.arange(orbitals.shape[0] * lax.axis_size("kq"), dtype=jnp.int32)
    pick_first = (numbers[:, None] == first_points[None, :]).astype(jnp.float32)
    pick_second = (numbers[:, None] == second_points[None, :]).astype(jnp.float32)
    first_term = jnp.einsum("cp,pnr->cnr", pick_first, first_share, precision=lax.Precision.HIGHEST)
    second_term = jnp.einsum(
        "cp,pnr->cnr", pick_second, toward_second, precision=lax.Precision.HIGHEST
    )
    return lax.psum_scatter(first_term + second_term, "kq", scatter_dimension=0, tiled=True)


def solution(mesh):
    in_specs = (P("kq", "band", None), P("kq", None, None), P(), P("kq"), P())
    out_specs = P("kq", "band", None)
    return jax.shard_map(shards, mesh=mesh, in_specs=in_specs, out_specs=out_specs, check_vma=False)
```

profile of v0, /device:TPU:0, one launch (start us, length us, event | category | flops | bytes accessed | tf_op | source)
XLA Modules:
  0.0 1275.1 jit_solution(6615732303375635659)
XLA Ops:
  8.6 1.2 broadcast_subtract_fusion
  10.5 125.8 %all-gather.2.cloned.1.call-done = bf16[128,8,4096]{2,1,0:T(8,128)(2,1)} async-done(((bf16[1,8,4096]{2,1,0:T(8,128)(2,1)}), bf16[128,8,4096]{2,1,0:T(8,128)(2,1)}) %all-gather.2.cloned.1.call-update) | async-done | bytes 8388624 | tf_op jit(solution)/shard_map/all_gather | solution.py:64
  136.4 12.2 fusion.41
  148.7 12.5 fusion.44
  161.1 2.0 all_gather.7
  163.3 322.6 %while.13 = (s32[]{:T(128)}, bf16[2,16,4096]{2,1,0:T(8,128)(2,1)}, f32[2,8,4096]{2,0,1:T(2,128)S(1)}, bf16[2,8,4096]{2,1,0:T(8,128)(2,1)S(1)}, bf16[2,16,4096]{2...) while((s32[]{:T(128)}, bf16[2,16,4096]{2,1,0:T(8,128)(2,1)}, ...), condition=%wide.region_1.2_spmd.clone, body=%wide.region_0.1_spmd.clone.sunk | while | flops 2589425664 | bytes 13951255 | solution.py:85
  177.3 1.3 dynamic_slice.45
  180.5 1.8 fusion.93
  182.3 74.7 %fusion.94 = bf16[128,1024]{1,0:T(8,128)(2,1)} fusion(s32[4096]{0:T(1024)} %get-tuple-element.283, s32[1024]{0:T(1024)S(1)} %get-tuple-element.284, s32[4096]{0:T(1024)} %get-tuple-element.281, s32[1024]{0:T(1024)S(1)} %get-tuple-element.282, s32[4096]{0:T(1024)} %get-tuple-element.279, s32[1024]{0:T(1024)S(1)} %get-tuple-element.280, ...), kind=kOutput, calls=%fused_computation.19.clone.2 | convolution fusion | flops 1427505152 | bytes 2813952 | tf_op jit(solution)/shard_map/while/body/eval_jaxpr/dot_general | solution.py:42
  257.0 72.3 %multiply_reduce_fusion.4 = (bf16[4096,16]{0,1:T(8,128)(2,1)S(1)}, bf16[128,4096]{1,0:T(8,128)(2,1)S(1)}) fusion(f32[4096,8]{0,1:T(8,128)S(1)} %get-tuple-element.234, bf16[128,1024]{1,0:T(8,128)(2,1)} %fusion.94, s32[4096]{0:T(1024)} %get-tuple-element.283, s32[1024]{0:T(1024)S(1)} %get-tuple-element.284, s32[4096]{0:T(1024)} %get-tuple-element.281, ...), kind=kOutput, calls=%fused_computation.15.clone.2 | convolution fusion | flops 1160183808 | bytes 1634304 | tf_op jit(solution)/shard_map/while/body/eval_jaxpr/dot_general | solution.py:45
  329.7 1.1 dynamic_update_slice.14
  331.5 1.3 dynamic_slice.45
  334.7 1.8 fusion.93
  336.5 74.7 %fusion.94 = bf16[128,1024]{1,0:T(8,128)(2,1)} fusion(s32[4096]{0:T(1024)} %get-tuple-element.283, s32[1024]{0:T(1024)S(1)} %get-tuple-element.284, s32[4096]{0:T(1024)} %get-tuple-element.281, s32[1024]{0:T(1024)S(1)} %get-tuple-element.282, s32[4096]{0:T(1024)} %get-tuple-element.279, s32[1024]{0:T(1024)S(1)} %get-tuple-element.280, ...), kind=kOutput, calls=%fused_computation.19.clone.2 | convolution fusion | flops 1427505152 | bytes 2813952 | tf_op jit(solution)/shard_map/while/body/eval_jaxpr/dot_general | solution.py:42
  411.2 72.3 %multiply_reduce_fusion.4 = (bf16[4096,16]{0,1:T(8,128)(2,1)S(1)}, bf16[128,4096]{1,0:T(8,128)(2,1)S(1)}) fusion(f32[4096,8]{0,1:T(8,128)S(1)} %get-tuple-element.234, bf16[128,1024]{1,0:T(8,128)(2,1)} %fusion.94, s32[4096]{0:T(1024)} %get-tuple-element.283, s32[1024]{0:T(1024)S(1)} %get-tuple-element.284, s32[4096]{0:T(1024)} %get-tuple-element.281, ...), kind=kOutput, calls=%fused_computation.15.clone.2 | convolution fusion | flops 1160183808 | bytes 1634304 | tf_op jit(solution)/shard_map/while/body/eval_jaxpr/dot_general | solution.py:45
  483.8 1.1 dynamic_update_slice.14
  485.9 1.2 copy.31
  487.1 0.9 copy.39
  488.0 10.0 reduce-scatter.7.cloned.1.call-done
  498.0 1.0 reshape.72
  499.0 3.0 fusion.47
  502.0 10.5 convolution_add_fusion
  512.6 17.7 %copy.18 = f32[128,8,4096]{2,1,0:T(8,128)} copy(f32[128,8,4096]{2,0,1:T(8,128)} %convolution_add_fusion) | data formatting | bytes 33554432 | tf_op jit(solution)/shard_map/add | solution.py:96
  530.3 737.9 %reduce-scatter.5.cloned.1.call-done = f32[1,8,4096]{2,1,0:T(8,128)} async-done(((f32[128,8,4096]{2,1,0:T(8,128)}), f32[1,8,4096]{2,1,0:T(8,128)}) %reduce-scatter.5.cloned.1.call-update) | async-done | bytes 131088 | tf_op jit(solution)/shard_map/reduce_scatter | solution.py:96
  (43 shorter events, 5.4 us)
Async XLA Ops:
  6.5 0.8 copy-start
  6.5 129.8 %all-gather.2.cloned.1.call-start = ((), (), s32[]{:S(2)}) async-start(), calls=%async_computation.2 | async-start | bytes 8454144 | tf_op jit(solution)/shard_map/all_gather | solution.py:64
  7.3 490.8 %reduce-scatter.7.cloned.1.call-start = ((), (), s32[]{:S(2)}) async-start(), calls=%async_computation.4 | async-start | bytes 393216
  9.8 126.5 %copy-start.5 = (s32[2]{0:T(128)}, s32[2]{0:T(128)S(1)}, u32[]{:S(2)}) copy-start(s32[2]{0:T(128)S(1)} %get-tuple-element.146) | copy-start | bytes 28
  9.8 153.4 %copy-start.4 = (s32[2]{0:T(128)}, s32[2]{0:T(128)S(1)}, u32[]{:S(2)}) copy-start(s32[2]{0:T(128)S(1)} %get-tuple-element.145) | copy-start | bytes 28
  257.0 73.7 %copy-start.2 = (bf16[2,16,4096]{2,1,0:T(8,128)(2,1)S(1)}, bf16[2,16,4096]{2,1,0:T(8,128)(2,1)}, u32[]{:S(2)}) copy-start(bf16[2,16,4096]{2,1,0:T(8,128)(2,1)} %get-tuple-element.257) | copy-start | bytes 786436 | tf_op jit(solution)/shard_map/while
  330.8 0.7 copy-start.3
  411.2 73.7 %copy-start.2 = (bf16[2,16,4096]{2,1,0:T(8,128)(2,1)S(1)}, bf16[2,16,4096]{2,1,0:T(8,128)(2,1)}, u32[]{:S(2)}) copy-start(bf16[2,16,4096]{2,1,0:T(8,128)(2,1)} %get-tuple-element.257) | copy-start | bytes 786436 | tf_op jit(solution)/shard_map/while
  485.0 0.7 copy-start.3
  485.9 16.2 %copy-start.6 = (s32[2]{0:T(128)S(1)}, s32[2]{0:T(128)}, u32[]{:S(2)}) copy-start(s32[2]{0:T(128)} %copy-done.5) | copy-start | bytes 28
  488.0 780.2 %reduce-scatter.5.cloned.1.call-start = ((), (), s32[]{:S(2)}) async-start(), calls=%async_computation.3 | async-start | bytes 16908288 | tf_op jit(solution)/shard_map/reduce_scatter | solution.py:96
  512.5 755.7 %copy-start.1 = (s32[256,2]{0,1:T(2,128)S(1)}, s32[256,2]{0,1:T(2,128)}, u32[]{:S(2)}) copy-start(s32[256,2]{0,1:T(2,128)} %param.9) | copy-start | bytes 6148
Sparse Core Ops, SparseCore 0:
  11.0 125.3 all-gather.1
  488.1 9.8 reduce-scatter.6
  530.4 737.7 reduce-scatter.4
where the time goes:
time: 1280 us
  waiting for transfers between devices  874 us (68%)
  matrix products  332 us (26%)
  local copies, waits for them, and re-layouts  31 us (2%)
  loops' own time  18.1 us (1%)
  between operations  13.6 us (1%)
    reduce_scatter x1, waiting for transfers between devices, shards(): lax.psum_scatter(first_term + second_term, 'kq', scatter_dimension=0, til...  738 us
    dot_general x2, matrix products, pair_fields(): jnp.dot(spectrum, screen_mat, preferred_element_type=jnp.float32)  149 us
    dot_general x2, matrix products, pair_fields(): jnp.dot(screened, table, preferred_element_type=jnp.float32) * factor  145 us
    all_gather x1, waiting for transfers between devices, shards(): shard_piece = lax.all_gather(orbitals, 'kq', axis=0, tiled=True)  126 us
  transfers between devices with their start and end apart: 3, of which 3 were waited for; matrix products, arithmetic and copies ran while one was open for 0% of the time, Pallas kernels for 0%

commit v1 on v0

v1 whole, which is shorter than its diff:
```python
import functools
import math

import jax
import jax.numpy as jnp
import numpy as np
from jax import lax
from jax.experimental import pallas as pl
from jax.experimental.pallas import tpu as pltpu
from jax.sharding import PartitionSpec as P

N = 128
CHUNKS = 32
NG = 1024
ROWS = 256
MESH = pl.DeviceIdType.MESH
F32 = jnp.float32
BF16 = jnp.bfloat16

_W = np.arange(1.0, 5.0)
_COEF = np.linalg.solve(
    np.stack([_W, _W**3, _W**5, _W**7], axis=1), math.sqrt(2.0) * np.sin(np.pi * _W / 8)
)
_COEF = [float(c) for c in _COEF]


def wrap(value, size):
    return jnp.where(value >= size, value - size, value)


def root2_cos(phase):
    phase = jnp.bitwise_and(phase, 15)
    w = (4 - jnp.minimum(phase, 16 - phase)).astype(F32)
    s = w * w
    return w * (_COEF[0] + s * (_COEF[1] + s * (_COEF[2] + s * _COEF[3])))


def remote(src, dst, send_sem, recv_sem, chip, core):
    return pltpu.make_async_remote_copy(
        src_ref=src,
        dst_ref=dst,
        send_sem=send_sem,
        recv_sem=recv_sem,
        device_id=(chip, core),
        device_id_type=MESH,
    )


def build_table(gmap_ref, table):
    lane = lax.broadcasted_iota(jnp.int32, (16, 128), 1)
    scale = math.sqrt(0.5)

    @pl.loop(0, NG // 128)
    def _(block):
        row = gmap_ref[pl.ds(block, 1), :].astype(F32)
        column = jnp.transpose(jnp.broadcast_to(row, (128, 128))).astype(jnp.int32)
        for sub in range(8):
            freq = column[sub * 16 : (sub + 1) * 16, :]
            freq_x = lax.shift_right_logical(freq, 8)
            freq_y = jnp.bitwise_and(lax.shift_right_logical(freq, 4), 15)
            freq_z = jnp.bitwise_and(freq, 15)
            cos1 = root2_cos(freq_x) * scale
            sin1 = root2_cos(freq_x - 4) * scale
            cos4 = root2_cos(freq_x * 4) * scale
            sin4 = root2_cos(freq_x * 4 - 4) * scale
            cos8 = (1 - 2 * jnp.bitwise_and(freq_x, 1)).astype(F32)
            rows = pl.ds(pl.multiple_of(block * 128 + sub * 16, 16), 16)
            for half in range(2):
                coord_y = half * 8 + lax.shift_right_logical(lane, 4)
                coord_z = jnp.bitwise_and(lane, 15)
                phase = freq_y * coord_y + freq_z * coord_z
                plus = root2_cos(phase - 2)
                minus = root2_cos(phase + 2)
                for x in range(4):
                    if x:
                        plus, minus = (
                            cos1 * plus + sin1 * minus,
                            cos1 * minus - sin1 * plus,
                        )
                    later = cos4 * plus + sin4 * minus
                    for step, value in (
                        (0, plus),
                        (8, cos8 * plus),
                        (4, later),
                        (12, cos8 * later),
                    ):
                        start = (x + step) * 256 + half * 128
                        table[rows, start : start + 128] = value.astype(BF16)


def compute(screen, slot, table, blocks, density, spectrum, screened, fields):
    def side(q, s):
        low = blocks[4 * q + s].astype(F32)
        high = blocks[4 * q + 2 + s].astype(F32)
        return jnp.concatenate([low, high], axis=0)

    @pl.loop(0, CHUNKS)
    def _(q):
        left, right = side(q, 0), side(q, 1)
        product = left[:, None, :] * right[None, :, :]
        lanes = pl.ds(pl.multiple_of(q * 128, 128), 128)
        density[:, lanes] = product.reshape(ROWS, 128).astype(BF16)

    @pl.loop(0, NG // 256)
    def _(t):
        rows = pl.ds(pl.multiple_of(t * 256, 256), 256)
        value = lax.dot_general(
            density[...], table[rows, :], (((1,), (1,)), ((), ())), preferred_element_type=F32
        )
        spectrum[:, rows] = (value * (1.0 / 64.0)).astype(BF16)

    @pl.loop(0, NG // 256)
    def _(t):
        columns = pl.ds(pl.multiple_of(t * 256, 256), 256)
        value = jnp.dot(spectrum[...], screen[slot, :, columns], preferred_element_type=F32)
        screened[:, columns] = (value * (1.0 / 64.0)).astype(BF16)

    @pl.loop(0, CHUNKS // 2)
    def _(t):
        lanes = pl.ds(pl.multiple_of(t * 256, 256), 256)
        value = jnp.dot(screened[...], table[:, lanes], preferred_element_type=F32)
        for h in range(2):
            q = 2 * t + h
            left, right = side(q, 0), side(q, 1)
            potential = value[:, h * 128 : (h + 1) * 128].reshape(16, 16, 128)
            first = jnp.sum(potential * right[None, :, :], axis=1).astype(BF16)
            second = jnp.sum(potential * left[:, None, :], axis=0).astype(BF16)
            fields[4 * q + 0] = first[0:8]
            fields[4 * q + 1] = second[0:8]
            fields[4 * q + 2] = first[8:16]
            fields[4 * q + 3] = second[8:16]


def kernel(
    pair_ref, q_ref, gmap_ref, x_ref, screening_ref, o_ref,
    gathered, outgoing, blocks, fields, returned, resorted, arrived,
    table, screen, density, spectrum, screened,
    send_sem, recv_sem, local_sem, entry_sem,
):
    me = lax.axis_index("kq")
    core = lax.axis_index("band")
    chunk = lax.div(me, 4)
    plane = lax.div(lax.rem(me, 4), 2)
    slot = lax.rem(me, 2)
    same = plane == core

    load = pltpu.make_async_copy(screening_ref, screen, local_sem.at[4])
    load.start()

    at_x, at_y, at_z = lax.div(me, 32), lax.rem(lax.div(me, 8), 4), lax.rem(me, 8)
    along_z = [at_x * 32 + at_y * 8 + lax.rem(at_z + i, 8) for i in (4, 3, 5, 2, 6, 1, 7)]
    along_y = [at_x * 32 + lax.rem(at_y + i, 4) * 8 + at_z for i in (2, 1, 3)]
    along_x = [lax.rem(at_x + i, 4) * 32 + at_y * 8 + at_z for i in (2, 1, 3)]
    barrier = pltpu.get_barrier_semaphore()

    def greet(sem, chip, to_core):
        pl.semaphore_signal(sem, inc=1, device_id=(chip, to_core), device_id_type=MESH)

    for chip in along_z + along_y + along_x:
        greet(barrier, chip, core)
    greet(barrier, me, 1 - core)
    pl.semaphore_wait(barrier, 14)
    for chip in along_y:
        greet(entry_sem.at[0], chip, core)
    pl.semaphore_wait(entry_sem.at[0], 3)
    for chip in along_x:
        greet(entry_sem.at[1], chip, core)
    pl.semaphore_wait(entry_sem.at[1], 3)
    greet(entry_sem.at[2], me, 1 - core)
    pl.semaphore_wait(entry_sem.at[2], 1)

    @pl.loop(0, CHUNKS)
    def _(i):
        q = wrap(chunk + i, CHUNKS)
        piece = x_ref.at[:, pl.ds(pl.multiple_of(q * 128, 128), 128)]
        for s in range(2):
            chip = 4 * q + 2 * core + s
            for c in range(2):
                here = jnp.logical_and(chip == me, c == core)

                @pl.when(here)
                def _():
                    pltpu.make_async_copy(piece, gathered.at[me], local_sem.at[0]).start()

                @pl.when(jnp.logical_not(here))
                def _():
                    remote(
                        piece, gathered.at[me], send_sem.at[0], recv_sem.at[0], chip, c
                    ).start()

    build_table(gmap_ref, table)

    def finish(phase, src, dst, local, count):
        if local is not None:
            pltpu.make_async_copy(src.at[me], dst.at[me], local_sem.at[phase]).wait()
        both = remote(
            src.at[pl.ds(0, count)], dst.at[pl.ds(0, count)],
            send_sem.at[phase], recv_sem.at[phase], me, core,
        )
        both.wait_send()
        both.wait_recv()

    @pl.when(same)
    def _():
        finish(0, gathered, gathered, True, N - 1)

    @pl.when(jnp.logical_not(same))
    def _():
        finish(0, gathered, gathered, None, N)

    shift = pair_ref[core, slot]

    @pl.loop(0, N, unroll=8)
    def _(o):
        outgoing[o] = gathered[wrap(o + shift, N)]

    def exchange(phase, src, dst):
        @pl.loop(1, N)
        def _(i):
            o = wrap(me + i, N)
            remote(src.at[o], dst.at[me], send_sem.at[phase], recv_sem.at[phase], o, core).start()

        pltpu.make_async_copy(src.at[me], dst.at[me], local_sem.at[phase]).start()

    exchange(1, outgoing, blocks)
    load.wait()
    finish(1, outgoing, blocks, True, N - 1)

    compute(screen, lax.rem(q_ref[core], 2), table, blocks, density, spectrum, screened, fields)

    exchange(2, fields, returned)
    finish(2, fields, returned, True, N - 1)

    @pl.loop(0, N, unroll=8)
    def _(k):
        resorted[k] = returned[wrap(k + N - shift, N)]

    place = 4 * chunk + 2 * slot + core

    @pl.loop(1, N)
    def _(i):
        k = wrap(me + i, N)
        remote(
            resorted.at[k], arrived.at[place], send_sem.at[3], recv_sem.at[3], k, plane
        ).start()

    def close(count):
        both = remote(
            resorted.at[pl.ds(0, count)], arrived.at[pl.ds(0, count)],
            send_sem.at[3], recv_sem.at[3], me, core,
        )
        both.wait_send()
        both.wait_recv()

    @pl.when(same)
    def _():
        own = pltpu.make_async_copy(resorted.at[me], arrived.at[place], local_sem.at[3])
        own.start()
        own.wait()
        close(N - 1)

    @pl.when(jnp.logical_not(same))
    def _():
        remote(
            resorted.at[me], arrived.at[place], send_sem.at[3], recv_sem.at[3], me, plane
        ).start()
        close(N)

    for q in range(CHUNKS):
        terms = [arrived[4 * q + j].astype(F32) for j in range(4)]
        o_ref[:, q * 128 : (q + 1) * 128] = (terms[0] + terms[1]) + (terms[2] + terms[3])


def shards(orbitals, screening, pair_k, pair_q, gmap):
    vmem = pl.BlockSpec(memory_space=pltpu.VMEM)
    smem = pl.BlockSpec(memory_space=pltpu.SMEM)
    piece = pltpu.VMEM((N, 8, 128), BF16)
    dma = pltpu.SemaphoreType.DMA
    field = pl.pallas_call(
        kernel,
        out_shape=jax.ShapeDtypeStruct((8, 4096), F32),
        in_specs=[smem, smem, vmem, vmem, pl.BlockSpec(memory_space=pl.ANY)],
        out_specs=vmem,
        scratch_shapes=[piece] * 7
        + [
            pltpu.VMEM((NG, 4096), BF16),
            pltpu.VMEM((2, NG, NG), BF16),
            pltpu.VMEM((ROWS, 4096), BF16),
            pltpu.VMEM((ROWS, NG), BF16),
            pltpu.VMEM((ROWS, NG), BF16),
            dma((4,)),
            dma((4,)),
            dma((5,)),
            pltpu.SemaphoreType.REGULAR((3,)),
        ],
        compiler_params=pltpu.CompilerParams(
            collective_id=0, has_side_effects=True, vmem_limit_bytes=48 << 20
        ),
    )(pair_k[:2], pair_q, gmap.reshape(8, 128), orbitals[0], screening)
    return field[None]


def solution(mesh):
    in_specs = (P("kq", "band", None), P("kq", None, None), P(), P("kq"), P())
    out_specs = P("kq", "band", None)
    return jax.shard_map(shards, mesh=mesh, in_specs=in_specs, out_specs=out_specs, check_vma=False)
```

time: 1280 us -> 72.2 us (0.06)
  the two profiles are of different devices: /device:TPU:0 before, /device:TPU:1 now
where the time goes in v1:
time: 72.2 us; the launch traced here: 72 us
  Pallas kernels  66.2 us (92%)
  local copies, waits for them, and re-layouts  5.8 us (8%)
    pallas_call x1, Pallas kernels, shards(): pl.pallas_call(kernel, out_shape=jax.ShapeDtypeStruct((8, 4096), F32), in...  66.2 us
    unnamed x10, local copies, waits for them, and re-layouts  5.12 us

profile of v1, /device:TPU:1, one launch (start us, length us, event | category | flops | bytes accessed | tf_op | source)
XLA Modules:
  0.0 72.0 jit_solution(717707455052378467)
XLA Ops:
  0.0 0.7 slice.3
  0.7 0.1 copy.7.pair_ref
  0.8 0.0 copy-start
  0.8 2.2 %copy-done = bf16[2,1024,1024]{2,1,0:T(8,128)(2,1)S(1)} copy-done((bf16[2,1024,1024]{2,1,0:T(8,128)(2,1)S(1)}, bf16[2,1024,1024]{2,1,0:T(8,128)(2,1)}, u32[]{:S(2)}) %copy-start) | copy-done | bytes 4194328
  3.0 0.0 copy-start.1
  3.0 0.8 %copy-done.1 = bf16[1,8,4096]{2,1,0:T(8,128)(2,1)S(1)} copy-done((bf16[1,8,4096]{2,1,0:T(8,128)(2,1)S(1)}, bf16[1,8,4096]{2,1,0:T(8,128)(2,1)}, u32[]{:S(2)}) %copy-start.1) | copy-done | bytes 65560
  3.8 0.0 copy-start.2
  3.8 0.7 copy-done.2
  4.5 0.0 copy-start.3
  4.5 0.7 copy-done.3
  5.1 66.2 %shard_map.55 = f32[8,4096]{1,0:T(8,128)S(1)} custom-call(s32[2,2]{1,0:T(2,128)S(1)} %copy.7.pair_ref, s32[2]{0:T(128)S(1)} %copy-done.3, s32[8,128]{1,0:T(8,128)S(1)} %bitcast.5, bf16[8,4096]{1,0:T(8,128)(2,1)S(1)} %bitcast.4, bf16[2,1024,1024]{2,1,0:T(8,128)(2,1)S(1)} %copy-done), custom_call_target="tpu_custom_call" | custom-call | tf_op jit(solution)/shard_map/pallas_call | solution.py:279
  71.3 0.7 copy.9
Async XLA Ops:
  0.8 2.2 %copy-start = (bf16[2,1024,1024]{2,1,0:T(8,128)(2,1)S(1)}, bf16[2,1024,1024]{2,1,0:T(8,128)(2,1)}, u32[]{:S(2)}) copy-start(bf16[2,1024,1024]{2,1,0:T(8,128)(2,1)} %screening_ref.1) | copy-start | bytes 12582916
  3.0 0.8 %copy-start.1 = (bf16[1,8,4096]{2,1,0:T(8,128)(2,1)S(1)}, bf16[1,8,4096]{2,1,0:T(8,128)(2,1)}, u32[]{:S(2)}) copy-start(bf16[1,8,4096]{2,1,0:T(8,128)(2,1)} %param.5) | copy-start | bytes 196612
  3.8 0.7 copy-start.2
  4.5 0.7 copy-start.3

commit v2 on v1

--- a/solution.py
+++ b/solution.py
@@ -88,52 +88,53 @@
                         table[rows, start : start + 128] = value.astype(BF16)
 
 
-def compute(screen, slot, table, blocks, density, spectrum, screened, fields):
-    def side(q, s):
-        low = blocks[4 * q + s].astype(F32)
-        high = blocks[4 * q + 2 + s].astype(F32)
-        return jnp.concatenate([low, high], axis=0)
-
+def side(blocks, q, s):
+    return jnp.concatenate([blocks[4 * q + b, s].astype(F32) for b in range(4)], axis=0)
+
+
+def stage_density(blocks, density):
     @pl.loop(0, CHUNKS)
     def _(q):
-        left, right = side(q, 0), side(q, 1)
+        left, right = side(blocks, q, 0), side(blocks, q, 1)
         product = left[:, None, :] * right[None, :, :]
         lanes = pl.ds(pl.multiple_of(q * 128, 128), 128)
         density[:, lanes] = product.reshape(ROWS, 128).astype(BF16)
 
-    @pl.loop(0, NG // 256)
-    def _(t):
-        rows = pl.ds(pl.multiple_of(t * 256, 256), 256)
-        value = lax.dot_general(
-            density[...], table[rows, :], (((1,), (1,)), ((), ())), preferred_element_type=F32
-        )
-        spectrum[:, rows] = (value * (1.0 / 64.0)).astype(BF16)
-
-    @pl.loop(0, NG // 256)
-    def _(t):
-        columns = pl.ds(pl.multiple_of(t * 256, 256), 256)
-        value = jnp.dot(spectrum[...], screen[slot, :, columns], preferred_element_type=F32)
-        screened[:, columns] = (value * (1.0 / 64.0)).astype(BF16)
-
-    @pl.loop(0, CHUNKS // 2)
-    def _(t):
-        lanes = pl.ds(pl.multiple_of(t * 256, 256), 256)
-        value = jnp.dot(screened[...], table[:, lanes], preferred_element_type=F32)
-        for h in range(2):
-            q = 2 * t + h
-            left, right = side(q, 0), side(q, 1)
-            potential = value[:, h * 128 : (h + 1) * 128].reshape(16, 16, 128)
-            first = jnp.sum(potential * right[None, :, :], axis=1).astype(BF16)
-            second = jnp.sum(potential * left[:, None, :], axis=0).astype(BF16)
-            fields[4 * q + 0] = first[0:8]
-            fields[4 * q + 1] = second[0:8]
-            fields[4 * q + 2] = first[8:16]
-            fields[4 * q + 3] = second[8:16]
+
+def stage_one(density, table, spectrum):
+    value = lax.dot_general(
+        density[...], table[...], (((1,), (1,)), ((), ())), preferred_element_type=F32
+    )
+    spectrum[...] = (value * (1.0 / 64.0)).astype(BF16)
+
+
+def stage_two(spectrum, screen, slot, screened):
+    value = jnp.dot(spectrum[...], screen[slot], preferred_element_type=F32)
+    screened[...] = (value * (1.0 / 64.0)).astype(BF16)
+
+
+def stage_three(screened, table, blocks, fields):
+    value = jnp.dot(screened[...], table[...], preferred_element_type=F32)
+    for q in range(CHUNKS):
+        left, right = side(blocks, q, 0), side(blocks, q, 1)
+        potential = value[:, q * 128 : (q + 1) * 128].reshape(16, 16, 128)
+        first = jnp.sum(potential * right[None, :, :], axis=1)
+        second = jnp.sum(potential * left[:, None, :], axis=0)
+        for b in range(4):
+            fields[4 * q + b, 0] = first[4 * b : 4 * b + 4].astype(BF16)
+            fields[4 * q + b, 1] = second[4 * b : 4 * b + 4].astype(BF16)
+
+
+def compute(screen, slot, table, blocks, density, spectrum, screened, fields):
+    stage_density(blocks, density)
+    stage_one(density, table, spectrum)
+    stage_two(spectrum, screen, slot, screened)
+    stage_three(screened, table, blocks, fields)
 
 
 def kernel(
     pair_ref, q_ref, gmap_ref, x_ref, screening_ref, o_ref,
-    gathered, outgoing, blocks, fields, returned, resorted, arrived,
+    pieces, gathered, outgoing, blocks, fields, returned, resorted, arrived,
     table, screen, density, spectrum, screened,
     send_sem, recv_sem, local_sem, entry_sem,
 ):
@@ -141,11 +142,15 @@
     core = lax.axis_index("band")
     chunk = lax.div(me, 4)
     plane = lax.div(lax.rem(me, 4), 2)
-    slot = lax.rem(me, 2)
     same = plane == core
 
     load = pltpu.make_async_copy(screening_ref, screen, local_sem.at[4])
     load.start()
+
+    for q in range(CHUNKS):
+        block = x_ref[:, q * 128 : (q + 1) * 128].astype(F32)
+        for h in range(2):
+            pieces[q, h] = block[4 * h : 4 * h + 4].astype(BF16)
 
     at_x, at_y, at_z = lax.div(me, 32), lax.rem(lax.div(me, 8), 4), lax.rem(me, 8)
     along_z = [at_x * 32 + at_y * 8 + lax.rem(at_z + i, 8) for i in (4, 3, 5, 2, 6, 1, 7)]
@@ -169,29 +174,52 @@
     greet(entry_sem.at[2], me, 1 - core)
     pl.semaphore_wait(entry_sem.at[2], 1)
 
-    @pl.loop(0, CHUNKS)
-    def _(i):
-        q = wrap(chunk + i, CHUNKS)
-        piece = x_ref.at[:, pl.ds(pl.multiple_of(q * 128, 128), 128)]
-        for s in range(2):
-            chip = 4 * q + 2 * core + s
-            for c in range(2):
-                here = jnp.logical_and(chip == me, c == core)
-
-                @pl.when(here)
-                def _():
-                    pltpu.make_async_copy(piece, gathered.at[me], local_sem.at[0]).start()
-
-                @pl.when(jnp.logical_not(here))
-                def _():
-                    remote(
-                        piece, gathered.at[me], send_sem.at[0], recv_sem.at[0], chip, c
-                    ).start()
+    def far_first(send):
+        for dz in (4, 3, 5, 2, 6, 1, 7):
+            z = lax.rem(at_z + dz, 8)
+
+            @pl.loop(0, 16)
+            def _(i):
+                x = lax.rem(at_x + 2 + lax.div(i, 4), 4)
+                y = lax.rem(at_y + 2 + lax.rem(i, 4), 4)
+                send(x * 32 + y * 8 + z)
+
+        @pl.loop(1, 16)
+        def _(i):
+            x = lax.rem(at_x + lax.div(i, 4), 4)
+            y = lax.rem(at_y + lax.rem(i, 4), 4)
+            send(x * 32 + y * 8 + at_z)
+
+    for e in (1, 0):
+        z_high = lax.rem(lax.div(at_z, 4) + e, 2)
+
+        @pl.loop(0, 16)
+        def _(i):
+            x = lax.rem(at_x + 2 + lax.div(i, 4), 4)
+            y = lax.rem(at_y + 2 + lax.rem(i, 4), 4)
+            q = x * 8 + y * 2 + z_high
+            for h in range(2):
+                chip = 4 * q + 2 * core + h
+                for c in range(2):
+                    here = jnp.logical_and(chip == me, c == core)
+
+                    @pl.when(here)
+                    def _():
+                        pltpu.make_async_copy(
+                            pieces.at[q, h], gathered.at[me], local_sem.at[0]
+                        ).start()
+
+                    @pl.when(jnp.logical_not(here))
+                    def _():
+                        remote(
+                            pieces.at[q, h], gathered.at[me],
+                            send_sem.at[0], recv_sem.at[0], chip, c,
+                        ).start()
 
     build_table(gmap_ref, table)
 
     def finish(phase, src, dst, local, count):
-        if local is not None:
+        if local:
             pltpu.make_async_copy(src.at[me], dst.at[me], local_sem.at[phase]).wait()
         both = remote(
             src.at[pl.ds(0, count)], dst.at[pl.ds(0, count)],
@@ -206,20 +234,22 @@
 
     @pl.when(jnp.logical_not(same))
     def _():
-        finish(0, gathered, gathered, None, N)
-
-    shift = pair_ref[core, slot]
+        finish(0, gathered, gathered, False, N)
+
+    shifts = [pair_ref[core, s] for s in range(2)]
 
     @pl.loop(0, N, unroll=8)
     def _(o):
-        outgoing[o] = gathered[wrap(o + shift, N)]
+        for s in range(2):
+            outgoing[o, s] = gathered[wrap(o + shifts[s], N)]
 
     def exchange(phase, src, dst):
-        @pl.loop(1, N)
-        def _(i):
-            o = wrap(me + i, N)
-            remote(src.at[o], dst.at[me], send_sem.at[phase], recv_sem.at[phase], o, core).start()
-
+        def send(chip):
+            remote(
+                src.at[chip], dst.at[me], send_sem.at[phase], recv_sem.at[phase], chip, core
+            ).start()
+
+        far_first(send)
         pltpu.make_async_copy(src.at[me], dst.at[me], local_sem.at[phase]).start()
 
     exchange(1, outgoing, blocks)
@@ -233,16 +263,18 @@
 
     @pl.loop(0, N, unroll=8)
     def _(k):
-        resorted[k] = returned[wrap(k + N - shift, N)]
-
-    place = 4 * chunk + 2 * slot + core
-
-    @pl.loop(1, N)
-    def _(i):
-        k = wrap(me + i, N)
+        first = returned[wrap(k + N - shifts[0], N), 0].astype(F32)
+        second = returned[wrap(k + N - shifts[1], N), 1].astype(F32)
+        resorted[k] = (first + second).astype(BF16)
+
+    place = 4 * chunk + 2 * lax.rem(me, 2) + core
+
+    def deliver(chip):
         remote(
-            resorted.at[k], arrived.at[place], send_sem.at[3], recv_sem.at[3], k, plane
+            resorted.at[chip], arrived.at[place], send_sem.at[3], recv_sem.at[3], chip, plane
         ).start()
+
+    far_first(deliver)
 
     def close(count):
         both = remote(
@@ -261,27 +293,29 @@
 
     @pl.when(jnp.logical_not(same))
     def _():
-        remote(
-            resorted.at[me], arrived.at[place], send_sem.at[3], recv_sem.at[3], me, plane
-        ).start()
+        deliver(me)
         close(N)
 
     for q in range(CHUNKS):
-        terms = [arrived[4 * q + j].astype(F32) for j in range(4)]
-        o_ref[:, q * 128 : (q + 1) * 128] = (terms[0] + terms[1]) + (terms[2] + terms[3])
+        for h in range(2):
+            terms = [arrived[4 * q + 2 * h + i].astype(F32) for i in range(2)]
+            o_ref[4 * h : 4 * h + 4, q * 128 : (q + 1) * 128] = terms[0] + terms[1]
 
 
 def shards(orbitals, screening, pair_k, pair_q, gmap):
     vmem = pl.BlockSpec(memory_space=pltpu.VMEM)
     smem = pl.BlockSpec(memory_space=pltpu.SMEM)
-    piece = pltpu.VMEM((N, 8, 128), BF16)
+    single = pltpu.VMEM((N, 4, 128), BF16)
+    double = pltpu.VMEM((N, 2, 4, 128), BF16)
     dma = pltpu.SemaphoreType.DMA
     field = pl.pallas_call(
         kernel,
         out_shape=jax.ShapeDtypeStruct((8, 4096), F32),
         in_specs=[smem, smem, vmem, vmem, pl.BlockSpec(memory_space=pl.ANY)],
         out_specs=vmem,
-        scratch_shapes=[piece] * 7
+        scratch_shapes=[pltpu.VMEM((CHUNKS, 2, 4, 128), BF16), single]
+        + [double] * 4
+        + [single] * 2
         + [
             pltpu.VMEM((NG, 4096), BF16),
             pltpu.VMEM((2, NG, NG), BF16),

time: 72.2 us -> 64.4 us (0.89)
  Pallas kernels: 66.2 us -> 58.3 us
    pallas_call x1, Pallas kernels: 66.2 us -> 58.3 us  [shards(): pl.pallas_call(kernel, out_shape=jax.ShapeDtypeStruct((8, 4096), F32), in...]
where the time goes in v2:
time: 64.4 us; the launch traced here: 64.2 us
  Pallas kernels  58.3 us (91%)
  local copies, waits for them, and re-layouts  5.8 us (9%)
    pallas_call x1, Pallas kernels, shards(): pl.pallas_call(kernel, out_shape=jax.ShapeDtypeStruct((8, 4096), F32), in...  58.3 us
    unnamed x10, local copies, waits for them, and re-layouts  5.12 us

profile of v2, /device:TPU:1, one launch (start us, length us, event | category | flops | bytes accessed | tf_op | source)
XLA Modules:
  0.0 64.2 jit_solution(18072260787116647946)
XLA Ops:
  0.0 0.7 %slice.3 = s32[2,2]{0,1:T(2,128)S(1)} slice(s32[256,2]{0,1:T(2,128)} %param.7), slice={[0:2], [0:2]} | slice | bytes 32 | tf_op jit(solution)/shard_map/slice | solution.py:333
  0.7 0.1 copy.7.pair_ref
  0.8 0.0 copy-start
  0.8 2.2 %copy-done = bf16[2,1024,1024]{2,1,0:T(8,128)(2,1)S(1)} copy-done((bf16[2,1024,1024]{2,1,0:T(8,128)(2,1)S(1)}, bf16[2,1024,1024]{2,1,0:T(8,128)(2,1)}, u32[]{:S(2)}) %copy-start) | copy-done | bytes 4194328
  3.0 0.0 copy-start.1
  3.0 0.8 %copy-done.1 = bf16[1,8,4096]{2,1,0:T(8,128)(2,1)S(1)} copy-done((bf16[1,8,4096]{2,1,0:T(8,128)(2,1)S(1)}, bf16[1,8,4096]{2,1,0:T(8,128)(2,1)}, u32[]{:S(2)}) %copy-start.1) | copy-done | bytes 65560
  3.8 0.0 copy-start.2
  3.8 0.7 %copy-done.2 = s32[1024]{0:T(1024)S(1)} copy-done((s32[1024]{0:T(1024)S(1)}, s32[1024]{0:T(1024)}, u32[]{:S(2)}) %copy-start.2) | copy-done | bytes 4120
  4.5 0.0 copy-start.3
  4.5 0.7 %copy-done.3 = s32[2]{0:T(128)S(1)} copy-done((s32[2]{0:T(128)S(1)}, s32[2]{0:T(128)}, u32[]{:S(2)}) %copy-start.3) | copy-done | bytes 32
  5.1 58.3 %shard_map.55 = f32[8,4096]{1,0:T(8,128)S(1)} custom-call(s32[2,2]{1,0:T(2,128)S(1)} %copy.7.pair_ref, s32[2]{0:T(128)S(1)} %copy-done.3, s32[8,128]{1,0:T(8,128)S(1)} %bitcast.5, bf16[8,4096]{1,0:T(8,128)(2,1)S(1)} %bitcast.4, bf16[2,1024,1024]{2,1,0:T(8,128)(2,1)S(1)} %copy-done), custom_call_target="tpu_custom_call" | custom-call | tf_op jit(solution)/shard_map/pallas_call | solution.py:311
  63.5 0.7 %copy.9 = f32[1,8,4096]{2,1,0:T(8,128)} copy(f32[1,8,4096]{2,1,0:T(8,128)S(1)} %bitcast.3) | data formatting | bytes 262144
Async XLA Ops:
  0.8 2.2 %copy-start = (bf16[2,1024,1024]{2,1,0:T(8,128)(2,1)S(1)}, bf16[2,1024,1024]{2,1,0:T(8,128)(2,1)}, u32[]{:S(2)}) copy-start(bf16[2,1024,1024]{2,1,0:T(8,128)(2,1)} %screening_ref.1) | copy-start | bytes 12582916
  3.0 0.8 %copy-start.1 = (bf16[1,8,4096]{2,1,0:T(8,128)(2,1)S(1)}, bf16[1,8,4096]{2,1,0:T(8,128)(2,1)}, u32[]{:S(2)}) copy-start(bf16[1,8,4096]{2,1,0:T(8,128)(2,1)} %param.5) | copy-start | bytes 196612
  3.8 0.7 %copy-start.2 = (s32[1024]{0:T(1024)S(1)}, s32[1024]{0:T(1024)}, u32[]{:S(2)}) copy-start(s32[1024]{0:T(1024)} %param.9) | copy-start | bytes 12292
  4.5 0.7 %copy-start.3 = (s32[2]{0:T(128)S(1)}, s32[2]{0:T(128)}, u32[]{:S(2)}) copy-start(s32[2]{0:T(128)} %q_ref.1) | copy-start | bytes 28

commit v3 on v2

--- a/solution.py
+++ b/solution.py
@@ -133,10 +133,10 @@
 
 
 def kernel(
-    pair_ref, q_ref, gmap_ref, x_ref, screening_ref, o_ref,
-    pieces, gathered, outgoing, blocks, fields, returned, resorted, arrived,
+    pair_hbm, q_hbm, gmap_hbm, x_hbm, screening_ref, o_ref,
+    pair_ref, q_ref, gmap_ref, x_ref, pieces, gathered, outgoing, blocks, fields, returned, resorted, arrived,
     table, screen, density, spectrum, screened,
-    send_sem, recv_sem, local_sem, entry_sem,
+    send_sem, recv_sem, local_sem, entry_sem, load_sem,
 ):
     me = lax.axis_index("kq")
     core = lax.axis_index("band")
@@ -144,14 +144,6 @@
     plane = lax.div(lax.rem(me, 4), 2)
     same = plane == core
 
-    load = pltpu.make_async_copy(screening_ref, screen, local_sem.at[4])
-    load.start()
-
-    for q in range(CHUNKS):
-        block = x_ref[:, q * 128 : (q + 1) * 128].astype(F32)
-        for h in range(2):
-            pieces[q, h] = block[4 * h : 4 * h + 4].astype(BF16)
-
     at_x, at_y, at_z = lax.div(me, 32), lax.rem(lax.div(me, 8), 4), lax.rem(me, 8)
     along_z = [at_x * 32 + at_y * 8 + lax.rem(at_z + i, 8) for i in (4, 3, 5, 2, 6, 1, 7)]
     along_y = [at_x * 32 + lax.rem(at_y + i, 4) * 8 + at_z for i in (2, 1, 3)]
@@ -164,6 +156,30 @@
     for chip in along_z + along_y + along_x:
         greet(barrier, chip, core)
     greet(barrier, me, 1 - core)
+
+    loads = [
+        pltpu.make_async_copy(src, dst, load_sem.at[i])
+        for i, (src, dst) in enumerate(
+            (
+                (x_hbm.at[0], x_ref),
+                (gmap_hbm, gmap_ref),
+                (pair_hbm, pair_ref),
+                (q_hbm, q_ref),
+            )
+        )
+    ]
+    load = pltpu.make_async_copy(screening_ref, screen, local_sem.at[4])
+    for copy in loads:
+        copy.start()
+    load.start()
+    loads[0].wait()
+    for q in range(CHUNKS):
+        block = x_ref[:, q * 128 : (q + 1) * 128].astype(F32)
+        for h in range(2):
+            pieces[q, h] = block[4 * h : 4 * h + 4].astype(BF16)
+    for copy in loads[1:]:
+        copy.wait()
+
     pl.semaphore_wait(barrier, 14)
     for chip in along_y:
         greet(entry_sem.at[0], chip, core)
@@ -174,47 +190,51 @@
     greet(entry_sem.at[2], me, 1 - core)
     pl.semaphore_wait(entry_sem.at[2], 1)
 
+    columns = [
+        lax.rem(at_x + 2 + i // 4, 4) * 32 + lax.rem(at_y + 2 + i % 4, 4) * 8
+        for i in range(16)
+    ]
+
     def far_first(send):
-        for dz in (4, 3, 5, 2, 6, 1, 7):
-            z = lax.rem(at_z + dz, 8)
-
-            @pl.loop(0, 16)
-            def _(i):
-                x = lax.rem(at_x + 2 + lax.div(i, 4), 4)
-                y = lax.rem(at_y + 2 + lax.rem(i, 4), 4)
-                send(x * 32 + y * 8 + z)
-
-        @pl.loop(1, 16)
+        @pl.loop(0, 7)
         def _(i):
-            x = lax.rem(at_x + lax.div(i, 4), 4)
-            y = lax.rem(at_y + lax.rem(i, 4), 4)
-            send(x * 32 + y * 8 + at_z)
+            half = lax.div(i + 1, 2)
+            z = lax.rem(at_z + 4 + (1 - 2 * lax.rem(i, 2)) * half, 8)
+            for column in columns:
+                send(column + z)
+
+        for i in range(16):
+            if i != 10:
+                send(columns[i] + at_z)
+
+    def scatter(q, h, chip, c):
+        remote(
+            pieces.at[q, h], gathered.at[me], send_sem.at[0], recv_sem.at[0], chip, c
+        ).start()
 
     for e in (1, 0):
         z_high = lax.rem(lax.div(at_z, 4) + e, 2)
-
-        @pl.loop(0, 16)
-        def _(i):
-            x = lax.rem(at_x + 2 + lax.div(i, 4), 4)
-            y = lax.rem(at_y + 2 + lax.rem(i, 4), 4)
-            q = x * 8 + y * 2 + z_high
+        for i in range(16):
+            chip0 = columns[i] + 4 * z_high + 2 * core
+            q = lax.div(chip0, 4)
             for h in range(2):
-                chip = 4 * q + 2 * core + h
-                for c in range(2):
-                    here = jnp.logical_and(chip == me, c == core)
-
-                    @pl.when(here)
-                    def _():
-                        pltpu.make_async_copy(
-                            pieces.at[q, h], gathered.at[me], local_sem.at[0]
-                        ).start()
-
-                    @pl.when(jnp.logical_not(here))
-                    def _():
-                        remote(
-                            pieces.at[q, h], gathered.at[me],
-                            send_sem.at[0], recv_sem.at[0], chip, c,
-                        ).start()
+                if e == 1 or i != 10:
+                    scatter(q, h, chip0 + h, 0)
+                    scatter(q, h, chip0 + h, 1)
+                    continue
+                away = chip0 + h != me
+
+                @pl.when(away)
+                def _():
+                    scatter(q, h, chip0 + h, 0)
+                    scatter(q, h, chip0 + h, 1)
+
+                @pl.when(jnp.logical_not(away))
+                def _():
+                    scatter(q, h, me, 1 - core)
+                    pltpu.make_async_copy(
+                        pieces.at[q, h], gathered.at[me], local_sem.at[0]
+                    ).start()
 
     build_table(gmap_ref, table)
 
@@ -236,7 +256,7 @@
     def _():
         finish(0, gathered, gathered, False, N)
 
-    shifts = [pair_ref[core, s] for s in range(2)]
+    shifts = [pair_ref[s, core] for s in range(2)]
 
     @pl.loop(0, N, unroll=8)
     def _(o):
@@ -304,16 +324,22 @@
 
 def shards(orbitals, screening, pair_k, pair_q, gmap):
     vmem = pl.BlockSpec(memory_space=pltpu.VMEM)
-    smem = pl.BlockSpec(memory_space=pltpu.SMEM)
     single = pltpu.VMEM((N, 4, 128), BF16)
     double = pltpu.VMEM((N, 2, 4, 128), BF16)
     dma = pltpu.SemaphoreType.DMA
     field = pl.pallas_call(
         kernel,
         out_shape=jax.ShapeDtypeStruct((8, 4096), F32),
-        in_specs=[smem, smem, vmem, vmem, pl.BlockSpec(memory_space=pl.ANY)],
+        in_specs=[pl.BlockSpec(memory_space=pltpu.HBM)] * 5,
         out_specs=vmem,
-        scratch_shapes=[pltpu.VMEM((CHUNKS, 2, 4, 128), BF16), single]
+        scratch_shapes=[
+            pltpu.SMEM((2, 256), jnp.int32),
+            pltpu.SMEM((2,), jnp.int32),
+            pltpu.VMEM((8, 128), jnp.int32),
+            pltpu.VMEM((8, 4096), BF16),
+            pltpu.VMEM((CHUNKS, 2, 4, 128), BF16),
+            single,
+        ]
         + [double] * 4
         + [single] * 2
         + [
@@ -326,11 +352,12 @@
             dma((4,)),
             dma((5,)),
             pltpu.SemaphoreType.REGULAR((3,)),
+            dma((4,)),
         ],
         compiler_params=pltpu.CompilerParams(
-            collective_id=0, has_side_effects=True, vmem_limit_bytes=48 << 20
+            collective_id=0, has_side_effects=True, vmem_limit_bytes=67043328
         ),
-    )(pair_k[:2], pair_q, gmap.reshape(8, 128), orbitals[0], screening)
+    )(pair_k.T, pair_q, gmap.reshape(8, 128), orbitals, screening)
     return field[None]
 
 

time: 64.4 us -> 59.2 us (0.919)
  local copies, waits for them, and re-layouts: 5.8 us -> 1.57 us
  Pallas kernels: 58.3 us -> 57.5 us
    unnamed x10 -> x1, local copies, waits for them, and re-layouts: 5.12 us -> 1.57 us
    pallas_call x1, Pallas kernels: 58.3 us -> 57.5 us  [shards(): pl.pallas_call(kernel, out_shape=jax.ShapeDtypeStruct((8, 4096), F32), in...]
    slice x1 -> x0, local copies, waits for them, and re-layouts: 0.68 us -> none  [shards(): pair_k[:2]]
where the time goes in v3:
time: 59.2 us; the launch traced here: 59.1 us
  Pallas kernels  57.5 us (97%)
  local copies, waits for them, and re-layouts  1.57 us (3%)
    pallas_call x1, Pallas kernels, shards(): pl.pallas_call(kernel, out_shape=jax.ShapeDtypeStruct((8, 4096), F32), in...  57.5 us
    unnamed x1, local copies, waits for them, and re-layouts  1.57 us

profile of v3, /device:TPU:1, one launch (start us, length us, event | category | flops | bytes accessed | tf_op | source)
XLA Modules:
  0.0 59.1 jit_solution(9900579052297014455)
XLA Ops:
  0.0 57.5 %shard_map.55 = f32[8,4096]{1,0:T(8,128)} custom-call(s32[2,256]{1,0:T(2,128)} %bitcast.5, s32[2]{0:T(128)} %q_hbm.1, s32[8,128]{1,0:T(8,128)} %bitcast.4, bf16[1,8,4096]{2,1,0:T(8,128)(2,1)} %x_hbm.1, bf16[2,1024,1024]{2,1,0:T(8,128)(2,1)} %screening_ref.1), custom_call_target="tpu_custom_call" | custom-call | tf_op jit(solution)/shard_map/pallas_call | solution.py:330
  57.5 1.6 %copy.7 = f32[1,8,4096]{2,1,0:T(8,128)} copy(f32[1,8,4096]{2,1,0:T(8,128)} %bitcast.3) | data formatting | bytes 262144

commit v4 on v3

--- a/solution.py
+++ b/solution.py
@@ -113,11 +113,14 @@
     screened[...] = (value * (1.0 / 64.0)).astype(BF16)
 
 
-def stage_three(screened, table, blocks, fields):
-    value = jnp.dot(screened[...], table[...], preferred_element_type=F32)
-    for q in range(CHUNKS):
+def stage_three(part, screened, table, blocks, fields):
+    half = CHUNKS // 2
+    lanes = slice(part * half * 128, (part + 1) * half * 128)
+    value = jnp.dot(screened[...], table[:, lanes], preferred_element_type=F32)
+    for i in range(half):
+        q = part * half + i
         left, right = side(blocks, q, 0), side(blocks, q, 1)
-        potential = value[:, q * 128 : (q + 1) * 128].reshape(16, 16, 128)
+        potential = value[:, i * 128 : (i + 1) * 128].reshape(16, 16, 128)
         first = jnp.sum(potential * right[None, :, :], axis=1)
         second = jnp.sum(potential * left[:, None, :], axis=0)
         for b in range(4):
@@ -125,11 +128,10 @@
             fields[4 * q + b, 1] = second[4 * b : 4 * b + 4].astype(BF16)
 
 
-def compute(screen, slot, table, blocks, density, spectrum, screened, fields):
+def compute(screen, slot, table, blocks, density, spectrum, screened):
     stage_density(blocks, density)
     stage_one(density, table, spectrum)
     stage_two(spectrum, screen, slot, screened)
-    stage_three(screened, table, blocks, fields)
 
 
 def kernel(
@@ -245,7 +247,6 @@
             src.at[pl.ds(0, count)], dst.at[pl.ds(0, count)],
             send_sem.at[phase], recv_sem.at[phase], me, core,
         )
-        both.wait_send()
         both.wait_recv()
 
     @pl.when(same)
@@ -276,9 +277,31 @@
     load.wait()
     finish(1, outgoing, blocks, True, N - 1)
 
-    compute(screen, lax.rem(q_ref[core], 2), table, blocks, density, spectrum, screened, fields)
-
-    exchange(2, fields, returned)
+    compute(screen, lax.rem(q_ref[core], 2), table, blocks, density, spectrum, screened)
+
+    def give(chip):
+        remote(
+            fields.at[chip], returned.at[me], send_sem.at[2], recv_sem.at[2], chip, core
+        ).start()
+
+    for part in range(2):
+        stage_three(part, screened, table, blocks, fields)
+        bases = [x * 32 + y * 8 for x in (2 * part, 2 * part + 1) for y in range(4)]
+
+        @pl.loop(0, 7)
+        def _(i):
+            half = lax.div(i + 1, 2)
+            z = lax.rem(at_z + 4 + (1 - 2 * lax.rem(i, 2)) * half, 8)
+            for base in bases:
+                give(base + z)
+
+        for base in bases:
+
+            @pl.when(base + at_z != me)
+            def _():
+                give(base + at_z)
+
+    pltpu.make_async_copy(fields.at[me], returned.at[me], local_sem.at[2]).start()
     finish(2, fields, returned, True, N - 1)
 
     @pl.loop(0, N, unroll=8)
@@ -296,13 +319,20 @@
 
     far_first(deliver)
 
+    def sent(phase, buffer, count):
+        part = buffer.at[pl.ds(0, count)]
+        remote(part, part, send_sem.at[phase], recv_sem.at[phase], me, core).wait_send()
+
     def close(count):
         both = remote(
             resorted.at[pl.ds(0, count)], arrived.at[pl.ds(0, count)],
             send_sem.at[3], recv_sem.at[3], me, core,
         )
+        sent(0, gathered, count)
+        sent(1, outgoing, N - 1)
+        sent(2, fields, N - 1)
+        both.wait_recv()
         both.wait_send()
-        both.wait_recv()
 
     @pl.when(same)
     def _():

time: 59.2 us -> 58.8 us (level)
  no operation moved by 1% of the time
where the time goes in v4:
time: 58.8 us; the launch traced here: 58.7 us
  Pallas kernels  57.1 us (97%)
  local copies, waits for them, and re-layouts  1.57 us (3%)
    pallas_call x1, Pallas kernels, shards(): pl.pallas_call(kernel, out_shape=jax.ShapeDtypeStruct((8, 4096), F32), in...  57.1 us
    unnamed x1, local copies, waits for them, and re-layouts  1.57 us

profile of v4, /device:TPU:1, one launch (start us, length us, event | category | flops | bytes accessed | tf_op | source)
XLA Modules:
  0.0 58.7 jit_solution(867207923226815966)
XLA Ops:
  0.0 57.1 %shard_map.55 = f32[8,4096]{1,0:T(8,128)} custom-call(s32[2,256]{1,0:T(2,128)} %bitcast.5, s32[2]{0:T(128)} %q_hbm.1, s32[8,128]{1,0:T(8,128)} %bitcast.4, bf16[1,8,4096]{2,1,0:T(8,128)(2,1)} %x_hbm.1, bf16[2,1024,1024]{2,1,0:T(8,128)(2,1)} %screening_ref.1), custom_call_target="tpu_custom_call" | custom-call | tf_op jit(solution)/shard_map/pallas_call | solution.py:360
  57.1 1.6 %copy.7 = f32[1,8,4096]{2,1,0:T(8,128)} copy(f32[1,8,4096]{2,1,0:T(8,128)} %bitcast.3) | data formatting | bytes 262144
